TPU v7x, 128 devices: a whole 4x4x4 slice. The times are simulated.
128 devices in a mesh: req: 32 (over x, z, core), tp: 4 (over y).
Axes of the slice: x: 4, y: 4, z: 4, core: 2. Of those that a mesh axis runs over, the one named last changes fastest.
Arguments:
- tokens: bfloat16 [1024, 2048], P('req'), may hold values from -6 to 6
- deal_order: int32 [1024], replicated, may hold values from 0 to 1023, as said below
- page_table: int32 [1024, 6], P('req'), may hold values from 0 to 1343, as said below
- lengths: int32 [1024], P('req'), may hold values from 1 to 768, as said below
- qkv_weight: bfloat16 [2048, 3, 2048], P(None, None, 'tp'), may hold values from -0.125 to 0.125
- out_weight: bfloat16 [2048, 2048], P('tp'), may hold values from -0.125 to 0.125
- up_weight: bfloat16 [2048, 4096], P(None, 'tp'), may hold values from -0.125 to 0.125
- down_weight: bfloat16 [4096, 2048], P('tp'), may hold values from -0.09375 to 0.09375
- key_cache: bfloat16 [2, 1344, 128, 2048], P(None, 'req', None, 'tp')
- value_cache: bfloat16 [2, 1344, 128, 2048], P(None, 'req', None, 'tp'), may hold values from -6 to 6
- attn_norm: float32 [2, 2048], replicated
- mlp_norm: float32 [2, 2048], replicated
Outputs:
- output: bfloat16 [1024, 2048], P('req')
Inputs may be any that keep to these rules, and one draw needn't show every extreme that they name: `deal_order`: A permutation: every request is placed in exactly one slot. Of the 32 requests in the slots s // 32 = d of one block d, at most 2 come from one source block of rows r // 32 = j, and some pair of blocks has exactly 2. `page_table`: row s holds the pages of the request in dealt slot s: its first ceil(lengths[s] / 128) entries are pages of the block s // 32 * 42 to s // 32 * 42 + 41, no page serves two slots, and the remaining entries repeat the row's first page. `lengths`: A request fills at most 6 pages; the slots s // 32 = d of one block d fill at most 42 pages together, and some block fills exactly that many.
All inputs are finite; a program needn't handle non-finite values.
Results may differ from a plain program's by a relative error of at most 0.034.
Values may be sent and summed in bfloat16 or wider, within the bound.
No kernel may reach another device: no remote copies, remote signals or barrier semaphores. Data moves between devices by JAX's collectives and lax.ppermute only.
A program may use at most 448 MiB of HBM per device.

v0:
```python
import math
import jax
import jax.numpy as jnp
from jax import lax
from jax.sharding import PartitionSpec as P

HD = 128
epsilon = 1e-06


def layer_norm(row_total, gain_bias):
    row_mean = jnp.mean(row_total, axis=-1, keepdims=True)
    centered = row_total - row_mean
    row_var = jnp.mean(centered * centered, axis=-1, keepdims=True)
    return (centered * lax.rsqrt(row_var + epsilon) * gain_bias[0] + gain_bias[1]).astype(
        jnp.bfloat16
    )


def post_norm(partial_term, residual, gain_bias):
    row_total = lax.psum(partial_term.astype(jnp.bfloat16), "tp").astype(
        jnp.float32
    ) + residual.astype(jnp.float32)
    return layer_norm(row_total, gain_bias)


def head_masks(feat_share, head_dim):
    head_count = feat_share // head_dim
    owner = jnp.arange(feat_share, dtype=jnp.int32) // head_dim
    return owner[None, :] == jnp.arange(head_count, dtype=jnp.int32)[:, None]


def spread_query(query_flat, mask):
    return jnp.where(mask[None, :, :], query_flat[:, None, :], jnp.zeros((), query_flat.dtype))


def own_scores(query_flat, key_new, mask, score_scale):
    product = query_flat.astype(jnp.float32) * key_new.astype(jnp.float32)
    return jnp.sum(jnp.where(mask[None, :, :], product[:, None, :], 0.0), axis=-1) * score_scale


def finish_mix(scores, own_score, value_new, mask, mix_fn):
    row_max = jnp.maximum(jnp.max(scores, axis=-1), own_score)
    exp_cache = jnp.exp(scores - row_max[..., None])
    exp_own = jnp.exp(own_score - row_max)
    row_total = jnp.sum(exp_cache, axis=-1) + exp_own
    cache_weights = (exp_cache / row_total[..., None]).astype(jnp.bfloat16)
    own_weight = (exp_own / row_total).astype(jnp.bfloat16).astype(jnp.float32)
    mixed_wide = mix_fn(cache_weights)
    mixed_cache = jnp.sum(jnp.where(mask[None, :, :], mixed_wide, 0.0), axis=1)
    own_spread = jnp.sum(jnp.where(mask[None, :, :], own_weight[:, :, None], 0.0), axis=1)
    return mixed_cache + own_spread * value_new.astype(jnp.float32)


def attend_pool(
    query_flat, key_new, value_new, key_pool, value_pool, local_table, lengths, score_scale, mask
):
    req_rows, feat_share = query_flat.shape
    pool_pages, page_len = (key_pool.shape[0], key_pool.shape[1])
    slot_count = local_table.shape[1]
    page_ids = jnp.arange(pool_pages, dtype=jnp.int32)
    slot_ids = jnp.arange(slot_count, dtype=jnp.int32)
    slot_used = slot_ids[None, :] * page_len < lengths[:, None]
    page_hit = (local_table[:, :, None] == page_ids[None, None, :]) & slot_used[:, :, None]
    start_pos = jnp.sum(jnp.where(page_hit, slot_ids[None, :, None] * page_len, 0), axis=1)
    is_owned = jnp.any(page_hit, axis=1)
    position = start_pos[:, :, None] + jnp.arange(page_len, dtype=jnp.int32)[None, None, :]
    is_valid = (is_owned[:, :, None] & (position < lengths[:, None, None])).reshape(
        req_rows, pool_pages * page_len
    )
    flat_keys = key_pool.reshape(pool_pages * page_len, feat_share)
    flat_values = value_pool.reshape(pool_pages * page_len, feat_share)
    query_wide = spread_query(query_flat, mask)
    scores = (
        jnp.einsum("rhf,tf->rht", query_wide, flat_keys, preferred_element_type=jnp.float32)
        * score_scale
    )
    scores = jnp.where(is_valid[:, None, :], scores, -jnp.inf)
    own_score = own_scores(query_flat, key_new, mask, score_scale)

    def mix_pool(cache_weights):
        return jnp.einsum(
            "rht,tf->rhf", cache_weights, flat_values, preferred_element_type=jnp.float32
        )

    return finish_mix(scores, own_score, value_new, mask, mix_pool)


def local(
    tokens,
    deal_order,
    page_table,
    lengths,
    qkv_weight,
    out_weight,
    up_weight,
    down_weight,
    key_cache,
    value_cache,
    attn_norm,
    mlp_norm,
):
    req_rows, model_width = tokens.shape
    tp_count = lax.axis_size("tp")
    req_index = lax.axis_index("req")
    feat_share = model_width // tp_count
    score_scale = 1.0 / math.sqrt(HD)
    mask = head_masks(feat_share, HD)
    dealt_here = lax.dynamic_slice_in_dim(deal_order, req_index * req_rows, req_rows)
    everyone = lax.all_gather(tokens, "req", axis=0, tiled=True)
    current = jnp.take(everyone, dealt_here, axis=0)
    pool_pages = key_cache.shape[1]
    local_table = page_table - req_index * pool_pages
    qkv_flat = qkv_weight.reshape(model_width, 3 * feat_share)
    for layer_index in range(key_cache.shape[0]):
        projected = jnp.dot(current, qkv_flat, preferred_element_type=jnp.float32).astype(
            jnp.bfloat16
        )
        query_flat = projected[:, :feat_share]
        key_new = projected[:, feat_share : 2 * feat_share]
        value_new = projected[:, 2 * feat_share :]
        key_pool = key_cache[layer_index]
        value_pool = value_cache[layer_index]
        attended = attend_pool(
            query_flat,
            key_new,
            value_new,
            key_pool,
            value_pool,
            local_table,
            lengths,
            score_scale,
            mask,
        )
        attended = attended.astype(jnp.bfloat16)
        attn_term = jnp.dot(attended, out_weight, preferred_element_type=jnp.float32)
        hidden = post_norm(attn_term, current, attn_norm)
        up_proj = jnp.dot(hidden, up_weight, preferred_element_type=jnp.float32)
        activated = jax.nn.gelu(up_proj, approximate=True).astype(jnp.bfloat16)
        down_term = jnp.dot(activated, down_weight, preferred_element_type=jnp.float32)
        current = post_norm(down_term, hidden, mlp_norm)
    request_count = deal_order.shape[0]
    inverse = (
        jnp.zeros_like(deal_order).at[deal_order].set(jnp.arange(request_count, dtype=jnp.int32))
    )
    inverse_here = lax.dynamic_slice_in_dim(inverse, req_index * req_rows, req_rows)
    returned = lax.all_gather(current, "req", axis=0, tiled=True)
    result = jnp.take(returned, inverse_here, axis=0)
    return result


def solution(mesh):
    in_specs = (
        P("req", None),
        P(),
        P("req", None),
        P("req"),
        P(None, None, "tp"),
        P("tp", None),
        P(None, "tp"),
        P("tp", None),
        P(None, "req", None, "tp"),
        P(None, "req", None, "tp"),
        P(),
        P(),
    )
    out_specs = P("req", None)
    return jax.shard_map(local, mesh=mesh, in_specs=in_specs, out_specs=out_specs, check_vma=False)
```

profile of v0, /device:TPU:1, one launch (start us, length us, event | category | flops | bytes accessed | tf_op | source)
XLA Modules:
  0.0 334.8 jit_solution(1223456797249646341)
XLA Ops:
  6.5 0.7 all-gather.3.cloned.1.call-update
  7.3 8.8 %copy.16 = bf16[2048,3,512]{0,2,1:T(8,128)(2,1)} copy(bf16[2048,3,512]{2,0,1:T(8,128)(2,1)} %param.18) | data formatting | bytes 12582912 | tf_op args[4]
  16.4 0.1 fusion.41
  16.5 0.1 select_reduce_fusion.4
  16.7 9.8 %fusion.77 = (bf16[1,42,128,512]{3,2,1,0:T(8,128)(2,1)}, bf16[1,42,128,512]{3,2,1,0:T(8,128)(2,1)}) fusion(bf16[2,42,128,512]{3,2,1,0:T(8,128)(2,1)} %param.22), kind=kLoop, calls=%fused_computation.147 | loop fusion | bytes 22020096 | tf_op jit(solution)/shard_map/slice | solution.py:122
  26.4 9.7 %fusion.78 = (bf16[1,42,128,512]{3,2,1,0:T(8,128)(2,1)}, bf16[1,42,128,512]{3,2,1,0:T(8,128)(2,1)}) fusion(bf16[2,42,128,512]{3,2,1,0:T(8,128)(2,1)} %param.23), kind=kLoop, calls=%fused_computation.148 | loop fusion | bytes 22020096 | tf_op jit(solution)/shard_map/slice | solution.py:123
  36.2 0.3 add.173
  36.4 0.3 and.65
  36.7 0.3 fusion.11
  37.0 22.6 %all-gather.3.cloned.1.call-done = bf16[1024,2048]{1,0:T(8,128)(2,1)} async-done(((bf16[32,2048]{1,0:T(8,128)(2,1)}), bf16[1024,2048]{1,0:T(8,128)(2,1)}) %all-gather.3.cloned.1.call-update) | async-done | bytes 4194320 | tf_op jit(solution)/shard_map/all_gather | solution.py:110
  59.7 3.5 %gather_fusion = bf16[32,2048]{1,0:T(8,128)(2,1)S(1)} fusion(bf16[1024,2048]{1,0:T(8,128)(2,1)} %all-gather.3.cloned.1.call-done, s32[1024]{0:T(1024)S(1)} %pad_clamp_fusion.1), kind=kCustom, calls=%fused_computation.clone | custom fusion | bytes 262272 | tf_op jit(solution)/shard_map/jit(_take)/gather | solution.py:111
  63.2 4.9 %convolution_convert_fusion.1 = bf16[32,1536]{1,0:T(8,128)(2,1)S(1)} fusion(bf16[2048,1536]{0,1:T(8,128)(2,1)} %bitcast.44, bf16[32,2048]{1,0:T(8,128)(2,1)S(1)} %gather_fusion, pred[32]{0:T(512)(128)(4,1)S(1)} %get-tuple-element.8), kind=kOutput, calls=%fused_computation.14 | convolution fusion | flops 201441280 | bytes 6520864 | tf_op jit(solution)/shard_map/dot_general | solution.py:116
  68.2 0.1 select_reduce_fusion.3
  68.3 2.0 fusion.81
  70.3 0.5 fusion.2
  70.9 0.1 select_reduce_fusion.2
  71.0 1.0 fusion.8
  72.1 1.1 convolution_convert_fusion.5
  73.3 38.0 %all-reduce.5.cloned.1.call-done = bf16[32,2048]{1,0:T(8,128)(2,1)} async-done(((bf16[32,2048]{1,0:T(8,128)(2,1)}), bf16[32,2048]{1,0:T(8,128)(2,1)}) %all-reduce.5.cloned.1.call-update) | async-done | bytes 131088 | tf_op jit(solution)/shard_map/psum | solution.py:21
  111.3 1.1 fusion.13
  112.5 1.1 multiply_reduce_fusion.3
  113.6 1.1 add_convert_fusion.3
  114.7 5.7 %convolution_convert_fusion.4 = bf16[32,2048]{1,0:T(8,128)(2,1)} fusion(bf16[1024,2048]{1,0:T(8,128)(2,1)} %param.21, bf16[32,2048]{1,0:T(8,128)(2,1)S(1)} %add_convert_fusion.3, bf16[2048,1024]{1,0:T(8,128)(2,1)} %param.20), kind=kOutput, calls=%fused_computation.17 | convolution fusion | flops 268795904 | bytes 8650752 | tf_op jit(solution)/shard_map/dot_general | solution.py:140
  120.5 0.2 all-reduce.9.cloned.1.call-start
  120.7 41.5 %all-reduce.7.cloned.1.call-done = bf16[32,2048]{1,0:T(8,128)(2,1)} async-done(((bf16[32,2048]{1,0:T(8,128)(2,1)}), bf16[32,2048]{1,0:T(8,128)(2,1)}) %all-reduce.7.cloned.1.call-update) | async-done | bytes 131088 | tf_op jit(solution)/shard_map/psum | solution.py:21
  162.2 1.0 fusion.15
  163.3 1.1 multiply_reduce_fusion.2
  164.4 1.0 add_convert_fusion.2
  165.4 4.9 %convolution_convert_fusion = bf16[32,1536]{1,0:T(8,128)(2,1)S(1)} fusion(bf16[32,2048]{1,0:T(8,128)(2,1)S(1)} %add_convert_fusion.2, bf16[2048,1536]{0,1:T(8,128)(2,1)} %bitcast.45), kind=kOutput, calls=%fused_computation.13 | convolution fusion | flops 201375744 | bytes 6520832 | tf_op jit(solution)/shard_map/dot_general | solution.py:116
  170.3 0.1 select_reduce_fusion.1
  170.5 4.7 %fusion.82 = (f32[32,4]{0,1:T(4,128)S(1)}, f32[32,4,5376]{2,0,1:T(8,128)S(1)}) fusion(bf16[5376,512,1]{1,0,2:T(8,128)(2,1)} %bitcast.46, pred[4,512]{1,0:T(4,128)(4,1)S(1)} %iota_compare_fusion.1, bf16[32,512]{1,0:T(8,128)(2,1)S(1)} %slice.67, pred[32,5376]{1,0:T(8,128)(4,1)S(1)} %fusion.11), kind=kOutput, calls=%fused_computation.152 | convolution fusion | flops 706772864 | bytes 8464896 | tf_op jit(solution)/shard_map/rhf,tf->rht/dot_general | solution.py:75
  175.1 0.5 fusion.3
  175.7 0.1 select_reduce_fusion
  175.8 1.0 fusion.9
  176.9 1.1 convolution_convert_fusion.3
  178.1 41.7 %all-reduce.9.cloned.1.call-done = bf16[32,2048]{1,0:T(8,128)(2,1)} async-done(((bf16[32,2048]{1,0:T(8,128)(2,1)}), bf16[32,2048]{1,0:T(8,128)(2,1)}) %all-reduce.9.cloned.1.call-update) | async-done | bytes 131088 | tf_op jit(solution)/shard_map/psum | solution.py:21
  219.7 1.0 fusion.17
  220.8 1.1 multiply_reduce_fusion.1
  221.9 1.0 add_convert_fusion.1
  222.9 5.7 %convolution_convert_fusion.2 = bf16[32,2048]{1,0:T(8,128)(2,1)} fusion(bf16[1024,2048]{1,0:T(8,128)(2,1)} %param.21, bf16[32,2048]{1,0:T(8,128)(2,1)S(1)} %add_convert_fusion.1, bf16[2048,1024]{1,0:T(8,128)(2,1)} %param.20), kind=kOutput, calls=%fused_computation.15 | convolution fusion | flops 268795904 | bytes 8650752 | tf_op jit(solution)/shard_map/dot_general | solution.py:140
  228.7 41.7 %all-reduce.11.cloned.1.call-done = bf16[32,2048]{1,0:T(8,128)(2,1)} async-done(((bf16[32,2048]{1,0:T(8,128)(2,1)}), bf16[32,2048]{1,0:T(8,128)(2,1)}) %all-reduce.11.cloned.1.call-update) | async-done | bytes 131088 | tf_op jit(solution)/shard_map/psum | solution.py:21
  270.4 1.0 fusion.19
  271.5 1.1 multiply_reduce_fusion
  272.6 1.7 add_convert_fusion
  274.3 4.3 %scatter_custom_fusion = s32[1024]{0:T(1024)S(1)} fusion(s32[1024]{0:T(1024)S(1)} %compare_select_fusion, s32[1024]{0:T(1024)S(1)} %iota.51, s32[]{:T(128)} %constant.32.clone.1), kind=kCustom, calls=%fused_computation.111 | custom fusion | bytes 4100 | tf_op jit(solution)/shard_map/scatter | solution.py:144
  278.7 45.0 %all-gather.5.cloned.1.call-done = bf16[1024,2048]{1,0:T(8,128)(2,1)} async-done(((bf16[32,2048]{1,0:T(8,128)(2,1)}), bf16[1024,2048]{1,0:T(8,128)(2,1)}) %all-gather.5.cloned.1.call-update) | async-done | bytes 4194320 | tf_op jit(solution)/shard_map/all_gather | solution.py:147
  323.7 3.5 %gather_fusion.1 = bf16[32,2048]{1,0:T(8,128)(2,1)S(1)} fusion(bf16[1024,2048]{1,0:T(8,128)(2,1)} %all-gather.5.cloned.1.call-done, s32[1024]{0:T(1024)S(1)} %pad_clamp_fusion), kind=kCustom, calls=%fused_computation.1.clone | custom fusion | bytes 262272 | tf_op jit(solution)/shard_map/jit(_take)/gather | solution.py:148
  327.2 0.7 broadcast_select_fusion
  (64 shorter events, 0.8 us)
Async XLA Ops:
  6.5 65.5 %copy-start = (bf16[512,2048]{1,0:T(8,128)(2,1)S(1)}, bf16[512,2048]{1,0:T(8,128)(2,1)}, u32[]{:S(2)}) copy-start(bf16[512,2048]{1,0:T(8,128)(2,1)} %param.19) | copy-start | bytes 6291460
  6.5 53.1 %all-gather.3.cloned.1.call-start = ((), (), s32[]{:S(2)}) async-start(), calls=%async_computation | async-start | bytes 4325376 | tf_op jit(solution)/shard_map/all_gather | solution.py:110
  7.3 104.1 %all-reduce.5.cloned.1.call-start = ((), (), s32[]{:S(2)}) async-start(), calls=%async_computation.1 | async-start | bytes 262144 | tf_op jit(solution)/shard_map/psum | solution.py:21
  7.3 8.9 %copy-start.4 = (s32[1024]{0:T(1024)S(1)}, s32[1024]{0:T(1024)}, u32[]{:S(2)}) copy-start(s32[1024]{0:T(1024)} %param.15) | copy-start | bytes 12292
  7.3 9.0 %copy-start.6 = (s32[32]{0:T(128)S(1)}, s32[32]{0:T(128)}, u32[]{:S(2)}) copy-start(s32[32]{0:T(128)} %param.17) | copy-start | bytes 388
  7.3 9.1 %copy-start.5 = (s32[32,6]{0,1:T(8,128)S(1)}, s32[32,6]{0,1:T(8,128)}, u32[]{:S(2)}) copy-start(s32[32,6]{0,1:T(8,128)} %param.16) | copy-start | bytes 2308
  63.2 5.1 %copy-start.1 = (bf16[1,42,128,512]{3,2,1,0:T(8,128)(2,1)S(1)}, bf16[1,42,128,512]{3,2,1,0:T(8,128)(2,1)}, u32[]{:S(2)}) copy-start(bf16[1,42,128,512]{3,2,1,0:T(8,128)(2,1)} %get-tuple-element.11) | copy-start | bytes 16515076
  68.1 2.9 slice-start.2
  68.3 2.7 slice-start.3
  71.0 2.3 copy-start.2
  73.2 89.0 %all-reduce.7.cloned.1.call-start = ((), (), s32[]{:S(2)}) async-start(), calls=%async_computation.2 | async-start | bytes 262144 | tf_op jit(solution)/shard_map/psum | solution.py:21
  114.7 6.0 %copy-start.3 = (f32[2,2048]{1,0:T(2,128)S(1)}, f32[2,2048]{1,0:T(2,128)}, u32[]{:S(2)}) copy-start(f32[2,2048]{1,0:T(2,128)} %param.25) | copy-start | bytes 49156
  120.5 99.3 %all-reduce.9.cloned.1.call-start = ((), (), s32[]{:S(2)}) async-start(), calls=%async_computation.3 | async-start | bytes 262144 | tf_op jit(solution)/shard_map/psum | solution.py:21
  165.4 10.4 %slice-start = ((s8[5505024]{0:T(1024)(128)(4,1)}), s8[4194304]{0:T(1024)(128)(4,1)S(1)}, s32[]{:S(2)}) async-start(s8[5505024]{0:T(1024)(128)(4,1)} %bitcast.48), calls=%async_computation.6 | async-start | bytes 8388608
  170.5 5.4 %slice-start.1 = ((s8[5505024]{0:T(1024)(128)(4,1)}), s8[1310720]{0:T(1024)(128)(4,1)S(1)}, s32[]{:S(2)}) async-start(s8[5505024]{0:T(1024)(128)(4,1)} %bitcast.48), calls=%async_computation.7 | async-start | bytes 2621440
  178.0 92.4 %all-reduce.11.cloned.1.call-start = ((), (), s32[]{:S(2)}) async-start(), calls=%async_computation.4 | async-start | bytes 262144 | tf_op jit(solution)/shard_map/psum | solution.py:21
  228.7 95.1 %all-gather.5.cloned.1.call-start = ((), (), s32[]{:S(2)}) async-start(), calls=%async_computation.5 | async-start | bytes 4325376 | tf_op jit(solution)/shard_map/all_gather | solution.py:147
Sparse Core Ops, SparseCore 0:
  9.6 50.0 all-gather.2
  73.3 37.9 all-reduce.4
  120.6 41.5 all-reduce.6
  178.1 41.5 all-reduce.8
  228.8 41.5 all-reduce.10
  274.4 49.2 all-gather.4
where the time goes:
time: 335 us
  waiting for transfers between devices  231 us (69%)
  local copies, waits for them, and re-layouts  40.3 us (12%)
  matrix products  32.2 us (10%)
  other arithmetic  16.7 us (5%)
  between operations  13.9 us (4%)
    psum x4, waiting for transfers between devices, post_norm(): lax.psum(partial_term.astype(jnp.bfloat16), 'tp').astype(jnp.float32)  163 us
    all_gather x1, waiting for transfers between devices, local(): returned = lax.all_gather(current, 'req', axis=0, tiled=True)  45 us
    all_gather x1, waiting for transfers between devices, local(): everyone = lax.all_gather(tokens, 'req', axis=0, tiled=True)  22.6 us
    dot_general x2, matrix products, local(): jnp.dot(activated, down_weight, preferred_element_type=jnp.float32)  11.4 us
    dot_general x2, matrix products, local(): jnp.dot(current, qkv_flat, preferred_element_type=jnp.float32)  9.8 us
    slice x1, local copies, waits for them, and re-layouts, local(): key_pool = key_cache[layer_index]  9.76 us
    slice x1, local copies, waits for them, and re-layouts, local(): value_pool = value_cache[layer_index]  9.75 us
    unnamed x23, local copies, waits for them, and re-layouts  8.92 us
  transfers between devices with their start and end apart: 6, of which 6 were waited for; matrix products, arithmetic and copies ran while one was open for 10% of the time, Pallas kernels for 0%

commit v1 on v0

--- a/solution.py
+++ b/solution.py
@@ -144,7 +144,10 @@
         jnp.zeros_like(deal_order).at[deal_order].set(jnp.arange(request_count, dtype=jnp.int32))
     )
     inverse_here = lax.dynamic_slice_in_dim(inverse, req_index * req_rows, req_rows)
-    returned = lax.all_gather(current, "req", axis=0, tiled=True)
+    n_dev = lax.axis_size("req")
+    blocks = jnp.stack([current for _ in range(n_dev)])
+    blocks = lax.all_to_all(blocks, "req", split_axis=0, concat_axis=0)
+    returned = jnp.concatenate(blocks, axis=0)
     result = jnp.take(returned, inverse_here, axis=0)
     return result
 

time: 335 us -> 350 us (1.045)
  starting transfers between devices: 0.39 us -> 10.1 us
    all_to_all x0 -> x1, waiting for transfers between devices: none -> 47.8 us  [local(): blocks = lax.all_to_all(blocks, 'req', split_axis=0, concat_axis=0)]
    all_gather x1 -> x0, waiting for transfers between devices: 45 us -> none  [local(): returned = lax.all_gather(current, 'req', axis=0, tiled=True)]
    all_to_all x0 -> x1, starting transfers between devices: none -> 9.79 us  [local(): blocks = lax.all_to_all(blocks, 'req', split_axis=0, concat_axis=0)]
where the time goes in v1:
time: 350 us; the launch traced here: 349 us
  waiting for transfers between devices  234 us (67%)
  local copies, waits for them, and re-layouts  42.8 us (12%)
  matrix products  32.2 us (9%)
  other arithmetic  16.1 us (5%)
  between operations  13.6 us (4%)
  starting transfers between devices  10.1 us (3%)
    psum x4, waiting for transfers between devices, post_norm(): lax.psum(partial_term.astype(jnp.bfloat16), 'tp').astype(jnp.float32)  163 us
    all_to_all x1, waiting for transfers between devices, local(): blocks = lax.all_to_all(blocks, 'req', split_axis=0, concat_axis=0)  47.8 us
    all_gather x1, waiting for transfers between devices, local(): everyone = lax.all_gather(tokens, 'req', axis=0, tiled=True)  22.6 us
    dot_general x2, matrix products, local(): jnp.dot(activated, down_weight, preferred_element_type=jnp.float32)  11.4 us
    dot_general x2, matrix products, local(): jnp.dot(current, qkv_flat, preferred_element_type=jnp.float32)  9.8 us
    all_to_all x1, starting transfers between devices, local(): blocks = lax.all_to_all(blocks, 'req', split_axis=0, concat_axis=0)  9.79 us
    slice x1, local copies, waits for them, and re-layouts, local(): key_pool = key_cache[layer_index]  9.76 us
    slice x1, local copies, waits for them, and re-layouts, local(): value_pool = value_cache[layer_index]  9.75 us
  transfers between devices with their start and end apart: 6, of which 6 were waited for; matrix products, arithmetic and copies ran while one was open for 10% of the time, Pallas kernels for 0%

profile of v1, /device:TPU:1, one launch (start us, length us, event | category | flops | bytes accessed | tf_op | source)
XLA Modules:
  0.0 348.9 jit_solution(10504656967697662062)
XLA Ops:
  6.5 0.7 all-gather.2.cloned.1.call-update
  7.3 8.8 %copy.16 = bf16[2048,3,512]{0,2,1:T(8,128)(2,1)} copy(bf16[2048,3,512]{2,0,1:T(8,128)(2,1)} %param.18) | data formatting | bytes 12582912 | tf_op args[4]
  16.4 0.1 fusion.41
  16.5 0.1 select_reduce_fusion.4
  16.7 9.8 %fusion.77 = (bf16[1,42,128,512]{3,2,1,0:T(8,128)(2,1)}, bf16[1,42,128,512]{3,2,1,0:T(8,128)(2,1)}) fusion(bf16[2,42,128,512]{3,2,1,0:T(8,128)(2,1)} %param.22), kind=kLoop, calls=%fused_computation.147 | loop fusion | bytes 22020096 | tf_op jit(solution)/shard_map/slice | solution.py:122
  26.4 9.7 %fusion.78 = (bf16[1,42,128,512]{3,2,1,0:T(8,128)(2,1)}, bf16[1,42,128,512]{3,2,1,0:T(8,128)(2,1)}) fusion(bf16[2,42,128,512]{3,2,1,0:T(8,128)(2,1)} %param.23), kind=kLoop, calls=%fused_computation.148 | loop fusion | bytes 22020096 | tf_op jit(solution)/shard_map/slice | solution.py:123
  36.2 0.3 add.173
  36.4 0.3 and.65
  36.7 0.3 fusion.11
  37.0 22.6 %all-gather.2.cloned.1.call-done = bf16[1024,2048]{1,0:T(8,128)(2,1)} async-done(((bf16[32,2048]{1,0:T(8,128)(2,1)}), bf16[1024,2048]{1,0:T(8,128)(2,1)}) %all-gather.2.cloned.1.call-update) | async-done | bytes 4194320 | tf_op jit(solution)/shard_map/all_gather | solution.py:110
  59.7 3.5 %gather_fusion = bf16[32,2048]{1,0:T(8,128)(2,1)S(1)} fusion(bf16[1024,2048]{1,0:T(8,128)(2,1)} %all-gather.2.cloned.1.call-done, s32[1024]{0:T(1024)S(1)} %pad_clamp_fusion.1), kind=kCustom, calls=%fused_computation.clone | custom fusion | bytes 262272 | tf_op jit(solution)/shard_map/jit(_take)/gather | solution.py:111
  63.2 4.9 %convolution_convert_fusion.1 = bf16[32,1536]{1,0:T(8,128)(2,1)S(1)} fusion(bf16[2048,1536]{0,1:T(8,128)(2,1)} %bitcast.45, bf16[32,2048]{1,0:T(8,128)(2,1)S(1)} %gather_fusion, pred[32]{0:T(512)(128)(4,1)S(1)} %get-tuple-element.8), kind=kOutput, calls=%fused_computation.14 | convolution fusion | flops 201441280 | bytes 6520864 | tf_op jit(solution)/shard_map/dot_general | solution.py:116
  68.2 0.1 select_reduce_fusion.3
  68.3 2.0 fusion.81
  70.3 0.5 fusion.2
  71.0 1.0 fusion.8
  72.1 1.1 convolution_convert_fusion.5
  73.3 38.0 %all-reduce.5.cloned.1.call-done = bf16[32,2048]{1,0:T(8,128)(2,1)} async-done(((bf16[32,2048]{1,0:T(8,128)(2,1)}), bf16[32,2048]{1,0:T(8,128)(2,1)}) %all-reduce.5.cloned.1.call-update) | async-done | bytes 131088 | tf_op jit(solution)/shard_map/psum | solution.py:21
  111.3 1.1 fusion.13
  112.5 1.1 multiply_reduce_fusion.3
  113.6 1.1 add_convert_fusion.3
  114.7 5.7 %convolution_convert_fusion.4 = bf16[32,2048]{1,0:T(8,128)(2,1)} fusion(bf16[1024,2048]{1,0:T(8,128)(2,1)} %param.21, bf16[32,2048]{1,0:T(8,128)(2,1)S(1)} %add_convert_fusion.3, bf16[2048,1024]{1,0:T(8,128)(2,1)} %param.20), kind=kOutput, calls=%fused_computation.17 | convolution fusion | flops 268795904 | bytes 8650752 | tf_op jit(solution)/shard_map/dot_general | solution.py:140
  120.5 0.2 all-reduce.9.cloned.1.call-start
  120.7 41.5 %all-reduce.7.cloned.1.call-done = bf16[32,2048]{1,0:T(8,128)(2,1)} async-done(((bf16[32,2048]{1,0:T(8,128)(2,1)}), bf16[32,2048]{1,0:T(8,128)(2,1)}) %all-reduce.7.cloned.1.call-update) | async-done | bytes 131088 | tf_op jit(solution)/shard_map/psum | solution.py:21
  162.2 1.0 fusion.15
  163.3 1.1 multiply_reduce_fusion.2
  164.4 1.0 add_convert_fusion.2
  165.4 4.9 %convolution_convert_fusion = bf16[32,1536]{1,0:T(8,128)(2,1)S(1)} fusion(bf16[32,2048]{1,0:T(8,128)(2,1)S(1)} %add_convert_fusion.2, bf16[2048,1536]{0,1:T(8,128)(2,1)} %bitcast.46), kind=kOutput, calls=%fused_computation.13 | convolution fusion | flops 201375744 | bytes 6520832 | tf_op jit(solution)/shard_map/dot_general | solution.py:116
  170.3 0.1 select_reduce_fusion.1
  170.5 4.7 %fusion.82 = (f32[32,4]{0,1:T(4,128)S(1)}, f32[32,4,5376]{2,0,1:T(8,128)S(1)}) fusion(bf16[5376,512,1]{1,0,2:T(8,128)(2,1)} %bitcast.47, pred[4,512]{1,0:T(4,128)(4,1)S(1)} %iota_compare_fusion.1, bf16[32,512]{1,0:T(8,128)(2,1)S(1)} %slice.67, pred[32,5376]{1,0:T(8,128)(4,1)S(1)} %fusion.11), kind=kOutput, calls=%fused_computation.152 | convolution fusion | flops 706772864 | bytes 8464896 | tf_op jit(solution)/shard_map/rhf,tf->rht/dot_general | solution.py:75
  175.1 0.5 fusion.3
  175.8 1.0 fusion.9
  176.9 1.1 convolution_convert_fusion.3
  178.1 41.7 %all-reduce.9.cloned.1.call-done = bf16[32,2048]{1,0:T(8,128)(2,1)} async-done(((bf16[32,2048]{1,0:T(8,128)(2,1)}), bf16[32,2048]{1,0:T(8,128)(2,1)}) %all-reduce.9.cloned.1.call-update) | async-done | bytes 131088 | tf_op jit(solution)/shard_map/psum | solution.py:21
  219.7 1.0 fusion.17
  220.8 1.1 multiply_reduce_fusion.1
  221.9 1.0 add_convert_fusion.1
  222.9 5.7 %convolution_convert_fusion.2 = bf16[32,2048]{1,0:T(8,128)(2,1)} fusion(bf16[1024,2048]{1,0:T(8,128)(2,1)} %param.21, bf16[32,2048]{1,0:T(8,128)(2,1)S(1)} %add_convert_fusion.1, bf16[2048,1024]{1,0:T(8,128)(2,1)} %param.20), kind=kOutput, calls=%fused_computation.15 | convolution fusion | flops 268795904 | bytes 8650752 | tf_op jit(solution)/shard_map/dot_general | solution.py:140
  228.7 41.7 %all-reduce.11.cloned.1.call-done = bf16[32,2048]{1,0:T(8,128)(2,1)} async-done(((bf16[32,2048]{1,0:T(8,128)(2,1)}), bf16[32,2048]{1,0:T(8,128)(2,1)}) %all-reduce.11.cloned.1.call-update) | async-done | bytes 131088 | tf_op jit(solution)/shard_map/psum | solution.py:21
  270.4 1.0 fusion.19
  271.5 1.1 multiply_reduce_fusion
  272.6 1.0 add_convert_fusion
  273.6 2.5 stack.2
  276.1 9.8 %all-to-all-start = ((bf16[32,32,2048]{2,1,0:T(8,128)(2,1)}), bf16[32,32,2048]{2,1,0:T(8,128)(2,1)}, u32[]{:S(2)}, u32[]{:S(2)}) async-start(bf16[32,32,2048]{2,1,0:T(8,128)(2,1)} %stack.2), calls=%async_computation | async-start | bytes 8388608 | tf_op jit(solution)/shard_map/all_to_all | solution.py:149
  285.9 4.3 %scatter_custom_fusion = s32[1024]{0:T(1024)S(1)} fusion(s32[1024]{0:T(1024)S(1)} %compare_select_fusion, s32[1024]{0:T(1024)S(1)} %iota.51, s32[]{:T(128)} %constant.32.clone.1), kind=kCustom, calls=%fused_computation.111 | custom fusion | bytes 4100 | tf_op jit(solution)/shard_map/scatter | solution.py:144
  290.3 47.8 %all-to-all-done = bf16[32,32,2048]{2,1,0:T(8,128)(2,1)} async-done(((bf16[32,32,2048]{2,1,0:T(8,128)(2,1)}), bf16[32,32,2048]{2,1,0:T(8,128)(2,1)}, u32[]{:S(2)}, u32[]{:S(2)}) %all-to-all-start) | async-done | bytes 4194336 | tf_op jit(solution)/shard_map/all_to_all | solution.py:149
  338.1 3.5 %gather_fusion.1 = bf16[32,2048]{1,0:T(8,128)(2,1)S(1)} fusion(bf16[1024,2048]{1,0:T(8,128)(2,1)} %bitcast.14, s32[1024]{0:T(1024)S(1)} %pad_clamp_fusion), kind=kCustom, calls=%fused_computation.1.clone | custom fusion | bytes 262272 | tf_op jit(solution)/shard_map/jit(_take)/gather | solution.py:151
  341.6 0.7 broadcast_select_fusion
  (64 shorter events, 0.9 us)
Async XLA Ops:
  6.5 65.5 %copy-start = (bf16[512,2048]{1,0:T(8,128)(2,1)S(1)}, bf16[512,2048]{1,0:T(8,128)(2,1)}, u32[]{:S(2)}) copy-start(bf16[512,2048]{1,0:T(8,128)(2,1)} %param.19) | copy-start | bytes 6291460
  6.5 53.1 %all-gather.2.cloned.1.call-start = ((), (), s32[]{:S(2)}) async-start(), calls=%async_computation.1 | async-start | bytes 4325376 | tf_op jit(solution)/shard_map/all_gather | solution.py:110
  7.3 104.1 %all-reduce.5.cloned.1.call-start = ((), (), s32[]{:S(2)}) async-start(), calls=%async_computation.2 | async-start | bytes 262144 | tf_op jit(solution)/shard_map/psum | solution.py:21
  7.3 8.9 %copy-start.4 = (s32[1024]{0:T(1024)S(1)}, s32[1024]{0:T(1024)}, u32[]{:S(2)}) copy-start(s32[1024]{0:T(1024)} %param.15) | copy-start | bytes 12292
  7.3 9.0 %copy-start.6 = (s32[32]{0:T(128)S(1)}, s32[32]{0:T(128)}, u32[]{:S(2)}) copy-start(s32[32]{0:T(128)} %param.17) | copy-start | bytes 388
  7.3 9.1 %copy-start.5 = (s32[32,6]{0,1:T(8,128)S(1)}, s32[32,6]{0,1:T(8,128)}, u32[]{:S(2)}) copy-start(s32[32,6]{0,1:T(8,128)} %param.16) | copy-start | bytes 2308
  63.2 5.1 %copy-start.1 = (bf16[1,42,128,512]{3,2,1,0:T(8,128)(2,1)S(1)}, bf16[1,42,128,512]{3,2,1,0:T(8,128)(2,1)}, u32[]{:S(2)}) copy-start(bf16[1,42,128,512]{3,2,1,0:T(8,128)(2,1)} %get-tuple-element.11) | copy-start | bytes 16515076
  68.1 2.9 slice-start.2
  68.3 2.7 slice-start.3
  71.0 2.3 copy-start.2
  73.2 89.0 %all-reduce.7.cloned.1.call-start = ((), (), s32[]{:S(2)}) async-start(), calls=%async_computation.3 | async-start | bytes 262144 | tf_op jit(solution)/shard_map/psum | solution.py:21
  114.7 6.0 %copy-start.3 = (f32[2,2048]{1,0:T(2,128)S(1)}, f32[2,2048]{1,0:T(2,128)}, u32[]{:S(2)}) copy-start(f32[2,2048]{1,0:T(2,128)} %param.25) | copy-start | bytes 49156
  120.5 99.3 %all-reduce.9.cloned.1.call-start = ((), (), s32[]{:S(2)}) async-start(), calls=%async_computation.4 | async-start | bytes 262144 | tf_op jit(solution)/shard_map/psum | solution.py:21
  165.4 10.4 %slice-start = ((s8[5505024]{0:T(1024)(128)(4,1)}), s8[4194304]{0:T(1024)(128)(4,1)S(1)}, s32[]{:S(2)}) async-start(s8[5505024]{0:T(1024)(128)(4,1)} %bitcast.49), calls=%async_computation.6 | async-start | bytes 8388608
  170.5 5.4 %slice-start.1 = ((s8[5505024]{0:T(1024)(128)(4,1)}), s8[1310720]{0:T(1024)(128)(4,1)S(1)}, s32[]{:S(2)}) async-start(s8[5505024]{0:T(1024)(128)(4,1)} %bitcast.49), calls=%async_computation.7 | async-start | bytes 2621440
  178.0 92.4 %all-reduce.11.cloned.1.call-start = ((), (), s32[]{:S(2)}) async-start(), calls=%async_computation.5 | async-start | bytes 262144 | tf_op jit(solution)/shard_map/psum | solution.py:21
  276.1 62.0 %all-to-all-start = ((bf16[32,32,2048]{2,1,0:T(8,128)(2,1)}), bf16[32,32,2048]{2,1,0:T(8,128)(2,1)}, u32[]{:S(2)}, u32[]{:S(2)}) async-start(bf16[32,32,2048]{2,1,0:T(8,128)(2,1)} %stack.2), calls=%async_computation | async-start | bytes 8388608 | tf_op jit(solution)/shard_map/all_to_all | solution.py:149
Sparse Core Ops, SparseCore 0:
  9.6 50.0 all-gather.1
  73.3 37.9 all-reduce.4
  120.6 41.5 all-reduce.6
  178.1 41.5 all-reduce.8
  228.8 41.5 all-reduce.10
